TPU v7x, 256 devices: a whole 4x4x8 slice. The times are simulated.
256 devices in a mesh: freq: 64 (over x, z, y_lo), panel: 4 (over y_hi, core).
Axes of the slice: x: 4, y: 4 (y_hi: 2, y_lo: 2; y = y_hi * 2 + y_lo), z: 8, core: 2. Of those that a mesh axis runs over, the one named last changes fastest.
Arguments:
- reflection: bfloat16 [2, 64, 1024, 1024], P(None, 'freq', None, 'panel'), may hold values from -0.1875 to 0.1875
- tile_mask: int32 [64, 16, 16], P('freq', None, 'panel'), may hold values 0 or 1
- focusing: bfloat16 [2, 64, 1024, 256], P(None, 'freq', 'panel'), may hold values from -6 to 6
- initial: float32 [2, 64, 1024, 256], P(None, 'freq', 'panel'), may hold values from -6 to 6
- onsets: int32 [1024, 256], P(('freq', 'panel')), may hold values from 1 to 64
Outputs:
- updated: float32 [2, 64, 1024, 256], P(None, 'freq', 'panel')
All inputs are finite; a program needn't handle non-finite values. No bound on the sum of `tile_mask` on one device may be relied on, other than what follows from the above.
Results may differ from a plain program's by a relative error of at most 0.0015.
Values may be sent and summed in bfloat16 or wider, within the bound.
No kernel may reach another device: no remote copies, remote signals or barrier semaphores. Data moves between devices by JAX's collectives and lax.ppermute only.
A program may use at most 64 MiB of HBM per device.

v0:
```python
import math
import jax
import jax.numpy as jnp
from jax import lax
from jax.sharding import PartitionSpec as P


def tables(length):
    counter = lax.iota(jnp.int32, length)
    product_mod = counter[:, None] * counter[None, :] % length
    angles = product_mod.astype(jnp.float32) * (2.0 * math.pi / length)
    return (jnp.cos(angles), jnp.sin(angles))


def exact_dot(operator_matrix, multiplied_input):
    return jnp.dot(
        operator_matrix,
        multiplied_input,
        precision=lax.Precision.HIGHEST,
        preferred_element_type=jnp.float32,
    )


def window_traces(traces, trace_onsets):
    length = traces.shape[1]
    trace_rows = traces.shape[3] * traces.shape[4]
    flat_rows = traces.reshape(2, length, trace_rows)
    cosine, sine = tables(length)
    real_t = (exact_dot(cosine, flat_rows[0]) - exact_dot(sine, flat_rows[1])) / length
    imaginary_trace_part = (
        exact_dot(sine, flat_rows[0]) + exact_dot(cosine, flat_rows[1])
    ) / length
    window = lax.iota(jnp.int32, length)[:, None] < trace_onsets.reshape(1, trace_rows)
    real_t = jnp.where(window, real_t, 0.0)
    imaginary_trace_part = jnp.where(window, imaginary_trace_part, 0.0)
    out_real = exact_dot(cosine, real_t) + exact_dot(sine, imaginary_trace_part)
    out_imag = exact_dot(cosine, imaginary_trace_part) - exact_dot(sine, real_t)
    return jnp.stack([out_real, out_imag]).astype(jnp.bfloat16).reshape(traces.shape)


def product(operator_matrix, multiplied_input):
    return jnp.einsum(
        "bqx,bxj->bqj", operator_matrix, multiplied_input, preferred_element_type=jnp.float32
    )


def contract(operator_matrix, multiplied_input):
    return jnp.einsum(
        "fabr,fabv->frv", operator_matrix, multiplied_input, preferred_element_type=jnp.float32
    )


def local(reflection, tile_mask, focusing, initial, onsets):
    per_device = reflection.shape[1]
    sources = reflection.shape[2]
    columns = reflection.shape[3]
    tile_edge_length = sources // tile_mask.shape[1]
    points = focusing.shape[3]
    filled = jnp.broadcast_to(
        tile_mask.astype(jnp.bfloat16)[:, :, None, :, None],
        (per_device, tile_mask.shape[1], tile_edge_length, tile_mask.shape[2], tile_edge_length),
    ).reshape(per_device, sources, columns)
    real_r = reflection[0] * filled
    imag_r = reflection[1] * filled
    real_g = product(real_r, focusing[0]) - product(imag_r, focusing[1])
    imag_g = product(real_r, focusing[1]) + product(imag_r, focusing[0])
    groups = lax.axis_size("freq")
    group_rows = sources // groups
    partial_g = jnp.stack([real_g, imag_g]).reshape(2, per_device, groups, group_rows, points)
    summed = lax.psum(partial_g, "panel")
    trace_onsets = lax.all_gather(onsets, "panel", axis=0, tiled=True)
    traces = lax.all_to_all(summed, "freq", split_axis=2, concat_axis=1, tiled=True)
    windowed = window_traces(traces, trace_onsets)
    returned_output = lax.all_to_all(windowed, "freq", split_axis=1, concat_axis=2, tiled=True)
    rows_real = real_r.reshape(per_device, groups, group_rows, columns)
    rows_imag = imag_r.reshape(per_device, groups, group_rows, columns)
    out_real = contract(rows_real, returned_output[0]) + contract(rows_imag, returned_output[1])
    out_imag = contract(rows_real, returned_output[1]) - contract(rows_imag, returned_output[0])
    return initial + jnp.stack([out_real, out_imag])


def solution(mesh):
    return jax.shard_map(
        local,
        mesh=mesh,
        in_specs=(
            P(None, "freq", None, "panel"),
            P("freq", None, "panel"),
            P(None, "freq", "panel", None),
            P(None, "freq", "panel", None),
            P(("freq", "panel"), None),
        ),
        out_specs=P(None, "freq", "panel", None),
        check_vma=False,
    )
```

profile of v0, /device:TPU:2, one launch (start us, length us, event | category | flops | bytes accessed | tf_op | source)
XLA Modules:
  0.0 195.2 jit_solution(1034007891396239297)
XLA Ops:
  6.5 0.0 copy-start
  6.5 0.0 all-reduce.2.cloned.1.call-start
  6.5 0.8 convert_bitcast_fusion
  7.3 0.1 copy.13
  7.4 0.3 broadcast_in_dim.19
  7.8 0.0 copy-start.1
  7.8 0.7 broadcast_in_dim.20
  8.4 0.0 copy-done
  8.4 0.1 slice_multiply_fusion.1
  8.5 0.2 copy-done.1
  8.7 0.3 fusion.12
  9.0 0.3 fusion.14
  9.3 0.3 convolution_add_fusion.2
  9.6 0.3 convolution_subtract_fusion.2
  9.9 1.5 pad_maximum_fusion
  11.4 0.0 all-reduce.2.cloned.1.call-update
  11.4 0.0 copy-start.3
  11.4 66.8 %all-reduce.2.cloned.1.call-done = f32[2,1,64,16,256]{4,3,1,0,2:T(8,128)} async-done(((f32[2,1,64,16,256]{4,3,1,0,2:T(8,128)}), f32[2,1,64,16,256]{4,3,1,0,2:T(8,128)}) %all-reduce.2.cloned.1.call-update) | async-done | bytes 2097168 | tf_op jit(solution)/shard_map/psum | solution.py:70
  78.3 10.6 %all-to-all-start = ((f32[2,1,64,16,256]{4,3,1,0,2:T(8,128)}), f32[2,1,64,16,256]{4,3,1,0,2:T(8,128)S(1)}, u32[]{:S(2)}, u32[]{:S(2)}) async-start(f32[2,1,64,16,256]{4,3,1,0,2:T(8,128)} %all-reduce.2.cloned.1.call-done), calls=%async_computation | async-start | bytes 4194304 | tf_op jit(solution)/shard_map/all_to_all | solution.py:72
  88.9 0.0 copy-done.3
  88.9 7.3 %all-gather = s32[4,4,256]{2,1,0:T(4,128)S(1)} all-gather(s32[1,4,256]{2,1,0:T(4,128)S(1)} %bitcast.114), channel_id=1, replica_groups=mesh['freq'=64,'panel'=4] {'panel'}, dimensions={0}, use_global_device_ids=true | all-gather | bytes 20480 | tf_op jit(solution)/shard_map/all_gather | solution.py:71
  96.1 43.7 %all-to-all-done = f32[2,1,64,16,256]{4,3,1,0,2:T(8,128)S(1)} async-done(((f32[2,1,64,16,256]{4,3,1,0,2:T(8,128)}), f32[2,1,64,16,256]{4,3,1,0,2:T(8,128)S(1)}, u32[]{:S(2)}, u32[]{:S(2)}) %all-to-all-start) | async-done | bytes 2097184 | tf_op jit(solution)/shard_map/all_to_all | solution.py:72
  139.8 0.2 fusion.76
  140.0 0.6 copy.35
  140.6 1.2 fusion.41
  141.8 1.2 fusion.37
  142.9 0.6 copy.36
  143.6 1.3 fusion.3
  144.8 1.2 fusion.2
  146.1 1.2 fusion.35
  147.2 1.2 fusion.32
  148.4 1.1 fusion.4
  149.6 1.2 fusion.5
  150.7 0.1 copy.38
  150.9 0.1 copy.37
  151.0 0.1 pad_maximum_fusion.1
  151.1 34.3 %all_to_all.8 = bf16[2,64,1,16,256]{4,3,2,0,1:T(8,128)(2,1)S(1)} all-to-all(bf16[2,64,1,16,256]{4,3,2,0,1:T(8,128)(2,1)S(1)} %pad_maximum_fusion.1), channel_id=1, replica_groups=mesh['freq'=64,'panel'=4] {'freq'}, dimensions={1} | all-to-all | bytes 2097152 | tf_op jit(solution)/shard_map/all_to_all | solution.py:74
  185.4 0.3 convolution_bitcast_fusion.2
  185.7 0.3 convolution_bitcast_fusion
  186.1 0.3 fusion.9
  186.4 0.0 copy-start.2
  186.4 0.3 fusion.7
  186.8 0.7 copy-done.2
  187.5 0.9 maximum_add_fusion
  (1 shorter events, 0.0 us)
Async XLA Ops:
  6.5 1.9 copy-start
  6.5 71.7 %all-reduce.2.cloned.1.call-start = ((), (), s32[]{:S(2)}) async-start(), calls=%async_computation.2 | async-start | bytes 4194304 | tf_op jit(solution)/shard_map/psum | solution.py:70
  7.8 1.0 copy-start.1
  11.4 77.4 %copy-start.3 = (s32[4,256]{1,0:T(4,128)S(1)}, s32[4,256]{1,0:T(4,128)}, u32[]{:S(2)}) copy-start(s32[4,256]{1,0:T(4,128)} %param.9) | copy-start | bytes 12292
  78.3 61.5 %all-to-all-start = ((f32[2,1,64,16,256]{4,3,1,0,2:T(8,128)}), f32[2,1,64,16,256]{4,3,1,0,2:T(8,128)S(1)}, u32[]{:S(2)}, u32[]{:S(2)}) async-start(f32[2,1,64,16,256]{4,3,1,0,2:T(8,128)} %all-reduce.2.cloned.1.call-done), calls=%async_computation | async-start | bytes 4194304 | tf_op jit(solution)/shard_map/all_to_all | solution.py:72
  186.4 1.0 copy-start.2
Sparse Core Ops, SparseCore 0:
  11.5 66.6 all-reduce.1
where the time goes:
time: 195 us
  waiting for transfers between devices  111 us (57%)
  blocking collectives  41.6 us (21%)
  between operations  13.6 us (7%)
  matrix products  12 us (6%)
  starting transfers between devices  10.6 us (5%)
  local copies, waits for them, and re-layouts  3.57 us (2%)
  other arithmetic  3.3 us (2%)
    psum x1, waiting for transfers between devices, local(): summed = lax.psum(partial_g, 'panel')  66.8 us
    all_to_all x1, waiting for transfers between devices, local(): lax.all_to_all(summed, 'freq', split_axis=2, concat_axis=1, tiled=True)  43.7 us
    all_to_all x1, blocking collectives, local(): lax.all_to_all(windowed, 'freq', split_axis=1, concat_axis=2, tiled=True)  34.3 us
    all_to_all x1, starting transfers between devices, local(): lax.all_to_all(summed, 'freq', split_axis=2, concat_axis=1, tiled=True)  10.6 us
    dot_general x8, matrix products, exact_dot(): jnp.dot(operator_matrix, multiplied_input, precision=lax.Precision.HIGHES...  9.47 us
    all_gather x1, blocking collectives, local(): trace_onsets = lax.all_gather(onsets, 'panel', axis=0, tiled=True)  7.27 us
  transfers between devices with their start and end apart: 2, of which 2 were waited for; matrix products, arithmetic and copies ran while one was open for 0% of the time, Pallas kernels for 0%

commit v1 on v0

--- a/solution.py
+++ b/solution.py
@@ -67,7 +67,7 @@
     groups = lax.axis_size("freq")
     group_rows = sources // groups
     partial_g = jnp.stack([real_g, imag_g]).reshape(2, per_device, groups, group_rows, points)
-    summed = lax.psum(partial_g, "panel")
+    summed = lax.all_gather(partial_g, "panel").sum(axis=0)
     trace_onsets = lax.all_gather(onsets, "panel", axis=0, tiled=True)
     traces = lax.all_to_all(summed, "freq", split_axis=2, concat_axis=1, tiled=True)
     windowed = window_traces(traces, trace_onsets)

time: 195 us -> 203 us (1.041)
  other arithmetic: 3.3 us -> 8.01 us
    all_gather x0 -> x1, waiting for transfers between devices: none -> 68 us  [local(): summed = lax.all_gather(partial_g, 'panel').sum(axis=0)]
    psum x1 -> x0, waiting for transfers between devices: 66.8 us -> none  [local(): summed = lax.psum(partial_g, 'panel')]
    reduce_sum x0 -> x1, other arithmetic: none -> 4.65 us  [local(): summed = lax.all_gather(partial_g, 'panel').sum(axis=0)]
where the time goes in v1:
time: 203 us
  waiting for transfers between devices  112 us (55%)
  blocking collectives  41.3 us (20%)
  between operations  13.6 us (7%)
  matrix products  12 us (6%)
  starting transfers between devices  10.7 us (5%)
  other arithmetic  8.01 us (4%)
  local copies, waits for them, and re-layouts  5.17 us (3%)
    all_gather x1, waiting for transfers between devices, local(): summed = lax.all_gather(partial_g, 'panel').sum(axis=0)  68 us
    all_to_all x1, waiting for transfers between devices, local(): lax.all_to_all(summed, 'freq', split_axis=2, concat_axis=1, tiled=True)  43.9 us
    all_to_all x1, blocking collectives, local(): lax.all_to_all(windowed, 'freq', split_axis=1, concat_axis=2, tiled=True)  34.2 us
    all_to_all x1, starting transfers between devices, local(): lax.all_to_all(summed, 'freq', split_axis=2, concat_axis=1, tiled=True)  10.7 us
    dot_general x8, matrix products, exact_dot(): jnp.dot(operator_matrix, multiplied_input, precision=lax.Precision.HIGHES...  9.46 us
    all_gather x1, blocking collectives, local(): trace_onsets = lax.all_gather(onsets, 'panel', axis=0, tiled=True)  7.15 us
    reduce_sum x1, other arithmetic, local(): summed = lax.all_gather(partial_g, 'panel').sum(axis=0)  4.65 us
  transfers between devices with their start and end apart: 2, of which 2 were waited for; matrix products, arithmetic and copies ran while one was open for 0% of the time, Pallas kernels for 0%

profile of v1, /device:TPU:2, one launch (start us, length us, event | category | flops | bytes accessed | tf_op | source)
XLA Modules:
  0.0 202.7 jit_solution(6182577591667766049)
XLA Ops:
  6.5 0.0 copy-start
  6.5 0.0 all-gather.3.cloned.1.call-start
  6.5 0.8 convert_bitcast_fusion
  7.3 0.1 copy.22
  7.4 0.3 broadcast_in_dim.19
  7.8 0.0 copy-start.1
  7.8 0.7 broadcast_in_dim.20
  8.4 0.0 copy-done
  8.4 0.1 slice_multiply_fusion.1
  8.5 0.2 copy-done.1
  8.7 0.3 fusion.14
  9.0 0.3 fusion.12
  9.3 0.3 convolution_subtract_fusion.2
  9.6 0.3 convolution_add_fusion.2
  9.9 1.5 pad_maximum_fusion
  11.5 0.0 all-gather.3.cloned.1.call-update
  11.5 68.0 %all-gather.3.cloned.1.call-done = f32[4,2,1,64,16,256]{5,4,3,2,1,0:T(8,128)} async-done(((f32[1,2,1,64,16,256]{5,4,3,2,1,0:T(8,128)}), f32[4,2,1,64,16,256]{5,4,3,2,1,0:T(8,128)}) %all-gather.3.cloned.1.call-update) | async-done | bytes 8388624 | tf_op jit(solution)/shard_map/all_gather | solution.py:70
  79.5 4.7 %reduce_sum.11 = f32[2,64,16,256]{3,2,1,0:T(8,128)S(1)} reduce(f32[4,2,1,64,16,256]{5,4,3,2,1,0:T(8,128)} %all-gather.3.cloned.1.call-done, f32[]{:T(128)} %constant.21.clone.1), dimensions={0,2}, to_apply=%region_0.0 | reduce | flops 1572864 | bytes 10485764 | tf_op jit(solution)/shard_map/reduce_sum | solution.py:70
  84.1 1.6 copy.23
  85.7 0.0 copy-start.3
  85.7 10.7 %all-to-all-start = ((f32[2,1,64,16,256]{4,3,0,1,2:T(8,128)}), f32[2,1,64,16,256]{4,3,0,1,2:T(8,128)S(1)}, u32[]{:S(2)}, u32[]{:S(2)}) async-start(f32[2,1,64,16,256]{4,3,0,1,2:T(8,128)} %copy.23), calls=%async_computation | async-start | bytes 4194304 | tf_op jit(solution)/shard_map/all_to_all | solution.py:72
  96.4 0.0 copy-done.3
  96.4 7.2 %all-gather = s32[4,4,256]{2,1,0:T(4,128)S(1)} all-gather(s32[1,4,256]{2,1,0:T(4,128)S(1)} %bitcast.114), channel_id=1, replica_groups=mesh['freq'=64,'panel'=4] {'panel'}, dimensions={0}, use_global_device_ids=true | all-gather | bytes 20480 | tf_op jit(solution)/shard_map/all_gather | solution.py:71
  103.6 43.9 %all-to-all-done = f32[2,1,64,16,256]{4,3,0,1,2:T(8,128)S(1)} async-done(((f32[2,1,64,16,256]{4,3,0,1,2:T(8,128)}), f32[2,1,64,16,256]{4,3,0,1,2:T(8,128)S(1)}, u32[]{:S(2)}, u32[]{:S(2)}) %all-to-all-start) | async-done | bytes 2097184 | tf_op jit(solution)/shard_map/all_to_all | solution.py:72
  147.5 0.2 fusion.76
  147.6 0.6 copy.31
  148.2 1.2 fusion.37
  149.4 1.1 fusion.41
  150.6 0.6 copy.32
  151.2 1.2 fusion.2
  152.4 1.2 fusion.35
  153.6 1.3 fusion.3
  154.9 1.2 fusion.32
  156.1 1.2 fusion.4
  157.2 0.1 copy.33
  157.3 1.2 fusion.5
  158.5 0.1 copy.34
  158.6 0.1 pad_maximum_fusion.1
  158.7 34.2 %all_to_all.8 = bf16[2,64,1,16,256]{4,3,2,0,1:T(8,128)(2,1)S(1)} all-to-all(bf16[2,64,1,16,256]{4,3,2,0,1:T(8,128)(2,1)S(1)} %pad_maximum_fusion.1), channel_id=1, replica_groups=mesh['freq'=64,'panel'=4] {'freq'}, dimensions={1} | all-to-all | bytes 2097152 | tf_op jit(solution)/shard_map/all_to_all | solution.py:74
  192.9 0.3 convolution_bitcast_fusion.2
  193.2 0.3 convolution_bitcast_fusion
  193.6 0.3 fusion.7
  193.9 0.0 copy-start.2
  193.9 0.3 fusion.9
  194.3 0.7 copy-done.2
  195.0 0.9 maximum_add_fusion
  (1 shorter events, 0.0 us)
Async XLA Ops:
  6.5 1.9 copy-start
  6.5 72.9 %all-gather.3.cloned.1.call-start = ((), (), s32[]{:S(2)}) async-start(), calls=%async_computation.2 | async-start | bytes 10485760 | tf_op jit(solution)/shard_map/all_gather | solution.py:70
  7.8 1.0 copy-start.1
  85.7 10.7 %copy-start.3 = (s32[4,256]{1,0:T(4,128)S(1)}, s32[4,256]{1,0:T(4,128)}, u32[]{:S(2)}) copy-start(s32[4,256]{1,0:T(4,128)} %param.9) | copy-start | bytes 12292
  85.7 61.8 %all-to-all-start = ((f32[2,1,64,16,256]{4,3,0,1,2:T(8,128)}), f32[2,1,64,16,256]{4,3,0,1,2:T(8,128)S(1)}, u32[]{:S(2)}, u32[]{:S(2)}) async-start(f32[2,1,64,16,256]{4,3,0,1,2:T(8,128)} %copy.23), calls=%async_computation | async-start | bytes 4194304 | tf_op jit(solution)/shard_map/all_to_all | solution.py:72
  193.9 1.0 copy-start.2
Sparse Core Ops, SparseCore 0:
  11.6 67.8 all-gather.2
